TPU v7x, 256 devices: a whole 4x4x8 slice. The times are simulated.
256 devices in a mesh: seq: 64 (over z, y, core), dp: 4 (over x).
Axes of the slice: x: 4, y: 4, z: 8, core: 2. Of those that a mesh axis runs over, the one named last changes fastest.
Arguments:
- inputs: bfloat16 [4, 16384, 512], P('dp', 'seq'), may hold values from -16 to 16
- write_vecs: bfloat16 [4, 16384, 128], P('dp', 'seq'), may hold values from -6 to 6
- read_vecs: bfloat16 [4, 16384, 128], P('dp', 'seq'), may hold values from -0.5 to 0.5
- dt_code: int32 [4, 8, 16384], P('dp', None, 'seq'), may hold values from 1 to 81920
- a_rate: float32 [8], replicated, may hold values from 0.4 to 682.6667
- w_out: bfloat16 [512, 2560], replicated, may hold values from -0.125 to 0.125
- grad_out: bfloat16 [4, 16384, 2560], P('dp', 'seq'), may hold values from -0.59765625 to 0.59765625
Outputs:
- outputs: bfloat16 [4, 16384, 512], P('dp', 'seq')
- grad_inputs: bfloat16 [4, 16384, 512], P('dp', 'seq')
- grad_write: bfloat16 [4, 16384, 128], P('dp', 'seq')
- grad_read: bfloat16 [4, 16384, 128], P('dp', 'seq')
- grad_w_out: float32 [512, 2560], P('seq')
All inputs are finite; a program needn't handle non-finite values.
Results may differ from a plain program's by a relative error of at most 0.0055.
Values sent between devices are 32-bit elements; how exact they have to be, the bound alone decides.
No kernel may reach another device: no remote copies, remote signals or barrier semaphores. Data moves between devices by JAX's collectives and lax.ppermute only.
A program may use at most 128 MiB of HBM per device.

v0:
```python
import jax
import jax.numpy as jnp
from jax import lax
from jax.sharding import PartitionSpec as P

HEAD_DIM = 64
STATE = 128
LOCAL_HEADS = 8
GROUP = 128
highest = lax.Precision.HIGHEST


def entering(part, axis, combine, identity, reverse):
    count = lax.axis_size(axis)
    place = lax.axis_index(axis)
    ahead = count - 1 - place if reverse else place
    gathered = jax.tree.map(lambda a: lax.all_gather(a, axis), part)
    state = jax.tree.map(lambda a, e: jnp.zeros_like(a) + jnp.asarray(e, a.dtype), part, identity)

    def one(step, state):
        source = count - 1 - step if reverse else step
        return combine(
            state, jax.tree.map(lambda a: lax.dynamic_index_in_dim(a, source, 0, False), gathered)
        )

    return lax.fori_loop(0, ahead, one, state)


def combine(first_part, second_part):
    return (
        first_part[0] * second_part[0],
        second_part[0][:, None, None] * first_part[1] + second_part[1],
    )


def shards(inputs, write_vecs, read_vecs, dt_code, a_rate, w_out, grad_out):
    tokens = inputs.shape[1]
    seq_len = tokens * lax.axis_size("seq")
    blocks = tokens // GROUP
    decay_rate = a_rate / (8.0 * seq_len)
    log_decay = -(decay_rate[:, None] * dt_code[0].astype(jnp.float32))
    weight = jnp.sqrt(-jnp.expm1(2.0 * log_decay))
    weight_rows = weight.reshape(LOCAL_HEADS, blocks, GROUP).transpose(1, 2, 0)[..., None]
    cum_decay = jnp.cumsum(log_decay.reshape(LOCAL_HEADS, blocks, GROUP), axis=2)
    group_last = cum_decay[:, :, -1]
    group_edges = jnp.cumsum(group_last, axis=1)
    totals = jnp.exp(group_edges[:, -1])
    before = jnp.concatenate(
        [jnp.zeros((LOCAL_HEADS, 1), jnp.float32), group_edges[:, :-1]], axis=1
    )
    end_decay = jnp.exp(group_edges[:, -1:] - group_edges)
    start_decay = jnp.exp(before)
    weighted = (
        inputs[0].astype(jnp.float32).reshape(blocks, GROUP, LOCAL_HEADS, HEAD_DIM) * weight_rows
    )
    b_half = write_vecs[0].reshape(blocks, GROUP, STATE)
    c_half = read_vecs[0].reshape(blocks, GROUP, STATE)
    b_rows = b_half.astype(jnp.float32)
    c_rows = c_half.astype(jnp.float32)
    rows_at = lax.broadcasted_iota(jnp.int32, (GROUP, GROUP), 0)
    cols_at = lax.broadcasted_iota(jnp.int32, (GROUP, GROUP), 1)
    spread = cum_decay[:, :, :, None] - cum_decay[:, :, None, :]
    decay_mask = jnp.exp(jnp.where((rows_at >= cols_at)[None, None], spread, -jnp.inf))
    scores = jnp.einsum("kin,kjn->kij", c_half, b_half, preferred_element_type=jnp.float32)
    mixed = decay_mask * scores[None]
    tail_decay = jnp.exp(group_last[:, :, None] - cum_decay)
    tail_rows = tail_decay.transpose(1, 2, 0)[..., None]
    head_decay = jnp.exp(cum_decay).transpose(1, 2, 0)[..., None]
    tailed = weighted * tail_rows
    group_states = jnp.einsum("kjhp,kjn->khpn", tailed, b_rows, precision=highest)
    block_row = lax.broadcasted_iota(jnp.int32, (blocks, blocks), 0)
    block_col = lax.broadcasted_iota(jnp.int32, (blocks, blocks), 1)
    fwd_weights = jnp.exp(
        jnp.where(
            (block_col < block_row)[None], before[:, :, None] - group_edges[:, None, :], -jnp.inf
        )
    )
    bwd_weights = jnp.exp(
        jnp.where(
            (block_col > block_row)[None], before[:, None, :] - group_edges[:, :, None], -jnp.inf
        )
    )
    local_in = jnp.einsum("hkm,mhpn->khpn", fwd_weights, group_states, precision=highest)
    own_state = jnp.einsum("hm,mhpn->hpn", end_decay, group_states, precision=highest)
    grad_rows = grad_out[0]
    grad_y = lax.dot_general(
        grad_rows, w_out, (((1,), (1,)), ((), ())), preferred_element_type=jnp.float32
    ).astype(jnp.bfloat16)
    grad_heads = grad_y.astype(jnp.float32).reshape(blocks, GROUP, LOCAL_HEADS, HEAD_DIM)
    grad_decayed = grad_heads * head_decay
    adj_groups = jnp.einsum("kihp,kin->khpn", grad_decayed, c_rows, precision=highest)
    own_adj = jnp.einsum("hm,mhpn->hpn", start_decay, adj_groups, precision=highest)
    identity = (
        jnp.ones((LOCAL_HEADS,), jnp.float32),
        jnp.zeros((LOCAL_HEADS, HEAD_DIM, STATE), jnp.float32),
    )
    carried_in = entering((totals, own_state), "seq", combine, identity, False)[1]
    adj_later = entering((totals, own_adj), "seq", combine, identity, True)[1]
    state_in = local_in + start_decay.T[:, :, None, None] * carried_in[None]
    y_intra = jnp.einsum("hkij,kjhp->kihp", mixed, weighted, precision=highest)
    y_inter = jnp.einsum("kin,khpn->kihp", c_rows, state_in, precision=highest) * head_decay
    outputs = (y_intra + y_inter).reshape(1, tokens, LOCAL_HEADS * HEAD_DIM).astype(jnp.bfloat16)
    adj_in = (
        jnp.einsum("hkm,mhpn->khpn", bwd_weights, adj_groups, precision=highest)
        + end_decay.T[:, :, None, None] * adj_later[None]
    )
    grad_weighted = jnp.einsum("hkij,kihp->kjhp", mixed, grad_heads, precision=highest)
    grad_weighted = grad_weighted + tail_rows * jnp.einsum(
        "khpn,kjn->kjhp", adj_in, b_rows, precision=highest
    )
    grad_inputs = (
        (grad_weighted * weight_rows)
        .reshape(1, tokens, LOCAL_HEADS * HEAD_DIM)
        .astype(jnp.bfloat16)
    )
    pair_dots = decay_mask * jnp.einsum("kihp,kjhp->hkij", grad_heads, weighted, precision=highest)
    grad_read = jnp.einsum("hkij,kjn->kin", pair_dots, b_rows, precision=highest)
    grad_read = grad_read + jnp.einsum("kihp,khpn->kin", grad_decayed, state_in, precision=highest)
    grad_write = jnp.einsum("hkij,kin->kjn", pair_dots, c_rows, precision=highest)
    grad_write = grad_write + jnp.einsum("kjhp,khpn->kjn", tailed, adj_in, precision=highest)
    grad_read = grad_read.reshape(1, tokens, STATE).astype(jnp.bfloat16)
    grad_write = grad_write.reshape(1, tokens, STATE).astype(jnp.bfloat16)
    out_rows = outputs[0]
    share = lax.psum_scatter(
        lax.dot_general(
            out_rows, grad_rows, (((0,), (0,)), ((), ())), preferred_element_type=jnp.float32
        ),
        "seq",
        scatter_dimension=0,
        tiled=True,
    )
    grad_w_out = lax.psum(share, "dp")
    return (outputs, grad_inputs, grad_write, grad_read, grad_w_out)


def solution(mesh):
    placed = (
        P("dp", "seq", None),
        P("dp", "seq", None),
        P("dp", "seq", None),
        P("dp", None, "seq"),
        P(),
        P(),
        P("dp", "seq", None),
    )
    return jax.shard_map(
        shards,
        mesh=mesh,
        in_specs=placed,
        out_specs=(
            P("dp", "seq", None),
            P("dp", "seq", None),
            P("dp", "seq", None),
            P("dp", "seq", None),
            P("seq", None),
        ),
        check_vma=False,
    )
```

profile of v0, /device:TPU:8, one launch (start us, length us, event | category | flops | bytes accessed | tf_op | source)
XLA Modules:
  0.0 548.1 jit_solution(9119124222800775612)
XLA Ops:
  10.4 2.2 reshape.165
  12.6 1.5 copy.90
  15.3 2.7 fusion.29
  19.5 2.2 fusion.11
  24.8 3.4 fusion.25
  36.1 128.3 %all-reduce.1 = f32[512]{0:T(512)} all-reduce(f32[512]{0:T(512)} %bitcast_dynamic-update-slice_fusion), channel_id=2, replica_groups=mesh['seq'=64,'dp'=4] {'seq'}, use_global_device_ids=true, to_apply=%add.1 | all-reduce | flops 512 | bytes 4096
  168.6 3.9 fusion.27
  172.5 4.1 fusion.31
  176.6 3.7 while.26
  180.4 1.6 fusion.8
  182.0 3.1 fusion.10
  186.1 3.2 fusion
  189.4 2.5 fusion.4
  191.9 2.8 convolution_bitcast_fusion.4
  194.7 25.9 %all-gather.8.cloned.1.call-done = f32[512,64,128]{2,1,0:T(8,128)} async-done(((f32[8,64,128]{2,1,0:T(8,128)}), f32[512,64,128]{2,1,0:T(8,128)}) %all-gather.8.cloned.1.call-update) | async-done | bytes 16777232 | tf_op jit(solution)/shard_map/all_gather | solution.py:17
  220.6 108.4 %while.27 = (s32[]{:T(128)}, f32[8,64,128]{2,1,0:T(8,128)S(1)}, s32[]{:T(128)}, f32[64,8]{1,0:T(8,128)}, f32[64,8,64,128]{3,2,1,0:T(8,128)}, /*index=5*/s32[]{:T(128)}, s32[]{:T(128)}, s32[]{:T(128)}, s32[]{:T(128)}) while((s32[]{:T(128)}, f32[8,64,128]{2,1,0:T(8,128)S(1)}, s32[]{:T(128)}, f32[64,8]{1,0:T(8,128)}, ...), condition=%wide.region_5.6_spmd, body=%wide.region_4.5_spmd.sunk | while | flops 131078 | bytes 786683 | solution.py:26
  329.0 2.2 convolution_bitcast_fusion.5
  331.2 1.9 fusion.15
  333.1 1.5 fusion.9
  335.5 157.6 %all-reduce.8.cloned.1.call-done = f32[512,2560]{1,0:T(8,128)} async-done(((f32[512,2560]{1,0:T(8,128)}), f32[512,2560]{1,0:T(8,128)}) %all-reduce.8.cloned.1.call-update) | async-done | bytes 5242896
  493.1 1.5 constant_dynamic-slice_fusion
  497.9 2.1 reshape.167
  501.0 39.1 %all-reduce.6.cloned.1.call-done = f32[8,2560]{1,0:T(8,128)} async-done(((f32[8,2560]{1,0:T(8,128)}), f32[8,2560]{1,0:T(8,128)}) %all-reduce.6.cloned.1.call-update) | async-done | bytes 81936 | tf_op jit(solution)/shard_map/psum | solution.py:132
  540.0 1.5 copy.187
  (208 shorter events, 136.1 us)
Async XLA Ops:
  7.2 12.3 %copy-start = (bf16[512,2560]{1,0:T(8,128)(2,1)S(1)}, bf16[512,2560]{1,0:T(8,128)(2,1)}, u32[]{:S(2)}) copy-start(bf16[512,2560]{1,0:T(8,128)(2,1)} %param.16) | copy-start | bytes 7864324
  7.2 6.9 %copy-start.7 = (bf16[1,256,128]{2,1,0:T(8,128)(2,1)S(1)}, bf16[1,256,128]{2,1,0:T(8,128)(2,1)}, u32[]{:S(2)}) copy-start(bf16[1,256,128]{2,1,0:T(8,128)(2,1)} %param.12) | copy-start | bytes 196612
  7.2 169.4 %all-gather.6.cloned.1.call-start = ((), (), s32[]{:S(2)}) async-start(), calls=%async_computation.1 | async-start | bytes 17039360 | tf_op jit(solution)/shard_map/all_gather | solution.py:17
  8.8 9.3 %copy-start.13 = (f32[2,128,8]{1,2,0:T(8,128)}, f32[2,128,8]{1,2,0:T(8,128)S(1)}, u32[]{:S(2)}) copy-start(f32[2,128,8]{1,2,0:T(8,128)S(1)} %get-tuple-element.170) | copy-start | bytes 24580
  9.4 8.7 %copy-start.11 = (f32[8,2,128]{2,0,1:T(8,128)}, f32[8,2,128]{2,0,1:T(8,128)S(1)}, u32[]{:S(2)}) copy-start(f32[8,2,128]{2,0,1:T(8,128)S(1)} %reduce_window_sum.24) | copy-start | bytes 24580
  9.6 8.5 %copy-start.15 = (f32[8,2]{0,1:T(2,128)}, f32[8,2]{0,1:T(2,128)S(1)}, u32[]{:S(2)}) copy-start(f32[8,2]{0,1:T(2,128)S(1)} %reduce_window_sum.26) | copy-start | bytes 196
  9.6 8.5 %copy-start.18 = (f32[8,1]{0,1:T(1,128)}, f32[8,1]{0,1:T(1,128)S(1)}, u32[]{:S(2)}) copy-start(f32[8,1]{0,1:T(1,128)S(1)} %get-tuple-element.179) | copy-start | bytes 100
  14.5 0.8 copy-start.3
  18.1 202.5 %all-gather.8.cloned.1.call-start = ((), (), s32[]{:S(2)}) async-start(), calls=%async_computation.2 | async-start | bytes 17039360 | tf_op jit(solution)/shard_map/all_gather | solution.py:17
  19.5 4.1 copy-start.8
  23.6 153.1 %copy-start.1 = (bf16[2,128,8,64]{1,0,3,2:T(2,128)(2,1)}, bf16[2,128,8,64]{1,0,3,2:T(2,128)(2,1)S(1)}, u32[]{:S(2)}) copy-start(bf16[2,128,8,64]{1,0,3,2:T(2,128)(2,1)S(1)} %reshape.143) | copy-start | bytes 786436
  24.0 0.8 copy-start.4
  28.2 464.9 %all-reduce.8.cloned.1.call-start = ((), (), s32[]{:S(2)}) async-start(), calls=%async_computation.3 | async-start | bytes 10485760
  180.4 5.7 %copy-start.5 = (bf16[1,256,2560]{2,1,0:T(8,128)(2,1)S(1)}, bf16[1,256,2560]{2,1,0:T(8,128)(2,1)}, u32[]{:S(2)}) copy-start(bf16[1,256,2560]{2,1,0:T(8,128)(2,1)} %param.17) | copy-start | bytes 3932164
  185.1 0.7 copy-start.6
  189.3 350.7 %all-reduce.6.cloned.1.call-start = ((), (), s32[]{:S(2)}) async-start(), calls=%async_computation | async-start | bytes 163840 | tf_op jit(solution)/shard_map/psum | solution.py:132
  194.7 134.3 %copy-start.14 = (f32[2,128,8]{1,2,0:T(8,128)S(1)}, f32[2,128,8]{1,2,0:T(8,128)}, u32[]{:S(2)}) copy-start(f32[2,128,8]{1,2,0:T(8,128)} %copy-done.13) | copy-start | bytes 24580
  329.0 5.6 %copy-start.2 = (bf16[2,128,8,64]{1,0,3,2:T(2,128)(2,1)S(1)}, bf16[2,128,8,64]{1,0,3,2:T(2,128)(2,1)}, u32[]{:S(2)}) copy-start(bf16[2,128,8,64]{1,0,3,2:T(2,128)(2,1)} %copy-done.1) | copy-start | bytes 786436
  329.0 5.6 %copy-start.12 = (f32[2,128,128]{2,1,0:T(8,128)S(1)}, f32[2,128,128]{2,1,0:T(8,128)}, u32[]{:S(2)}) copy-start(f32[2,128,128]{2,1,0:T(8,128)} %fusion.75) | copy-start | bytes 393220
  329.0 5.6 %copy-start.16 = (pred[128,128]{1,0:T(8,128)(4,1)S(1)}, pred[128,128]{1,0:T(8,128)(4,1)}, u32[]{:S(2)}) copy-start(pred[128,128]{1,0:T(8,128)(4,1)} %iota_compare_fusion) | copy-start | bytes 49156
  329.0 5.6 %copy-start.17 = (f32[8,2,128]{2,1,0:T(2,128)S(1)}, f32[8,2,128]{2,1,0:T(2,128)}, u32[]{:S(2)}) copy-start(f32[8,2,128]{2,1,0:T(2,128)} %copy.91) | copy-start | bytes 24580
  331.2 163.5 %copy-start.9 = (f32[2,128,128]{2,1,0:T(8,128)S(1)}, f32[2,128,128]{2,1,0:T(8,128)}, u32[]{:S(2)}) copy-start(f32[2,128,128]{2,1,0:T(8,128)} %fusion.4) | copy-start | bytes 393220
  331.2 163.5 %copy-start.10 = (f32[2,128,128]{2,1,0:T(8,128)S(1)}, f32[2,128,128]{2,1,0:T(8,128)}, u32[]{:S(2)}) copy-start(f32[2,128,128]{2,1,0:T(8,128)} %convolution_bitcast_fusion.4) | copy-start | bytes 393220
Sparse Core Ops, SparseCore 0:
  18.2 101.8 all-gather.5
  123.5 97.0 all-gather.7
  224.2 268.8 all-reduce.7
  495.9 44.1 all-reduce.5
where the time goes:
time: 553 us; the launch traced here: 548 us
  waiting for transfers between devices  223 us (40%)
  blocking collectives  128 us (23%)
  local copies, waits for them, and re-layouts  71.4 us (13%)
  other arithmetic  70 us (13%)
  matrix products  38.5 us (7%)
  between operations  15.4 us (3%)
    unnamed x5, waiting for transfers between devices  158 us
    unnamed x1, blocking collectives  128 us
    add x63, other arithmetic, combine(): second_part[0][:, None, None] * first_part[1] + second_part[1]  66.4 us
    mul x63, local copies, waits for them, and re-layouts, combine(): second_part[0][:, None, None] * first_part[1] + second_part[1]  43.9 us
    psum x1, waiting for transfers between devices, shards(): grad_w_out = lax.psum(share, 'dp')  39.1 us
    all_gather x2, waiting for transfers between devices, entering(): gathered = jax.tree.map(lambda a: lax.all_gather(a, axis), part)  25.9 us
    unnamed x48, local copies, waits for them, and re-layouts  15.5 us
  transfers between devices with their start and end apart: 4, of which 3 were waited for; matrix products, arithmetic and copies ran while one was open for 30% of the time, Pallas kernels for 0%

commit v1 on v0

--- a/solution.py
+++ b/solution.py
@@ -129,7 +129,7 @@
         scatter_dimension=0,
         tiled=True,
     )
-    grad_w_out = lax.psum(share, "dp")
+    grad_w_out = jnp.sum(lax.all_gather(share, "dp"), axis=0)
     return (outputs, grad_inputs, grad_write, grad_read, grad_w_out)
 
 

time: 553 us -> 524 us (0.948)
  waiting for transfers between devices: 223 us -> 179 us
  blocking collectives: 128 us -> 142 us
    psum x1 -> x0, waiting for transfers between devices: 39.1 us -> none  [shards(): grad_w_out = lax.psum(share, 'dp')]
    all_gather x0 -> x1, blocking collectives: none -> 13 us  [shards(): grad_w_out = jnp.sum(lax.all_gather(share, 'dp'), axis=0)]
    unnamed x5 -> x4, waiting for transfers between devices: 158 us -> 153 us
    unnamed x48 -> x43, local copies, waits for them, and re-layouts: 15.5 us -> 16.7 us
  transfers between devices with their start and end apart: 4 -> 3, of which waited for: 3 -> 2; matrix products, arithmetic and copies ran while one was open for 30% -> 32% of each run, Pallas kernels for 0% -> 0%
where the time goes in v1:
time: 524 us; the launch traced here: 519 us
  waiting for transfers between devices  179 us (34%)
  blocking collectives  142 us (27%)
  local copies, waits for them, and re-layouts  72.8 us (14%)
  other arithmetic  69.9 us (13%)
  matrix products  38.5 us (7%)
  between operations  15.4 us (3%)
    unnamed x4, waiting for transfers between devices  153 us
    unnamed x1, blocking collectives  129 us
    add x63, other arithmetic, combine(): second_part[0][:, None, None] * first_part[1] + second_part[1]  66.4 us
    mul x63, local copies, waits for them, and re-layouts, combine(): second_part[0][:, None, None] * first_part[1] + second_part[1]  43.9 us
    all_gather x2, waiting for transfers between devices, entering(): gathered = jax.tree.map(lambda a: lax.all_gather(a, axis), part)  26.5 us
    unnamed x43, local copies, waits for them, and re-layouts  16.7 us
    all_gather x1, blocking collectives, shards(): grad_w_out = jnp.sum(lax.all_gather(share, 'dp'), axis=0)  13 us
  transfers between devices with their start and end apart: 3, of which 2 were waited for; matrix products, arithmetic and copies ran while one was open for 32% of the time, Pallas kernels for 0%

profile of v1, /device:TPU:8, one launch (start us, length us, event | category | flops | bytes accessed | tf_op | source)
XLA Modules:
  0.0 519.3 jit_solution(3956154625152621726)
XLA Ops:
  10.3 2.1 reshape.166
  12.5 1.5 copy.90
  15.3 2.7 fusion.29
  19.3 2.2 fusion.11
  24.6 3.4 fusion.25
  36.1 128.5 %all-reduce.1 = f32[512]{0:T(512)} all-reduce(f32[512]{0:T(512)} %bitcast_dynamic-update-slice_fusion), channel_id=2, replica_groups=mesh['seq'=64,'dp'=4] {'seq'}, use_global_device_ids=true, to_apply=%add.1 | all-reduce | flops 512 | bytes 4096
  168.2 2.3 fusion.4
  171.3 4.0 fusion.27
  175.3 2.9 fusion.31
  178.2 3.6 while.26
  181.8 1.5 fusion.8
  183.3 3.1 fusion.10
  187.4 2.0 copy.127
  189.4 4.6 fusion
  194.0 26.5 %all-gather.9.cloned.1.call-done = f32[512,64,128]{2,1,0:T(8,128)} async-done(((f32[8,64,128]{2,1,0:T(8,128)}), f32[512,64,128]{2,1,0:T(8,128)}) %all-gather.9.cloned.1.call-update) | async-done | bytes 16777232 | tf_op jit(solution)/shard_map/all_gather | solution.py:17
  220.5 108.6 %while.27 = (s32[]{:T(128)}, f32[8,64,128]{2,1,0:T(8,128)S(1)}, s32[]{:T(128)}, f32[64,8]{1,0:T(8,128)}, f32[64,8,64,128]{3,2,1,0:T(8,128)}, /*index=5*/s32[]{:T(128)}, s32[]{:T(128)}, s32[]{:T(128)}, s32[]{:T(128)}) while((s32[]{:T(128)}, f32[8,64,128]{2,1,0:T(8,128)S(1)}, s32[]{:T(128)}, f32[64,8]{1,0:T(8,128)}, ...), condition=%wide.region_5.6_spmd, body=%wide.region_4.5_spmd.sunk | while | flops 131078 | bytes 786683 | solution.py:26
  330.6 2.5 fusion.14
  333.1 2.0 copy.128
  335.1 2.1 reshape.168
  337.2 2.1 reshape.167
  339.3 2.2 convolution_bitcast_fusion.4
  341.5 2.3 convolution_bitcast_fusion.5
  345.6 152.7 %all-reduce.5.cloned.1.call-done = f32[512,2560]{1,0:T(8,128)} async-done(((f32[512,2560]{1,0:T(8,128)}), f32[512,2560]{1,0:T(8,128)}) %all-reduce.5.cloned.1.call-update) | async-done | bytes 5242896
  499.1 13.0 %all-gather.3 = f32[32,2560]{1,0:T(8,128)S(1)} all-gather(f32[8,2560]{1,0:T(8,128)S(1)} %constant_dynamic-slice_fusion), channel_id=5, replica_groups=mesh['seq'=64,'dp'=4] {'dp'}, dimensions={0}, use_global_device_ids=true | all-gather | bytes 409600 | tf_op jit(solution)/shard_map/all_gather | solution.py:132
  (202 shorter events, 135.8 us)
Async XLA Ops:
  7.2 12.2 %copy-start = (bf16[512,2560]{1,0:T(8,128)(2,1)S(1)}, bf16[512,2560]{1,0:T(8,128)(2,1)}, u32[]{:S(2)}) copy-start(bf16[512,2560]{1,0:T(8,128)(2,1)} %param.16) | copy-start | bytes 7864324
  7.2 6.8 %copy-start.8 = (bf16[1,256,128]{2,1,0:T(8,128)(2,1)S(1)}, bf16[1,256,128]{2,1,0:T(8,128)(2,1)}, u32[]{:S(2)}) copy-start(bf16[1,256,128]{2,1,0:T(8,128)(2,1)} %param.12) | copy-start | bytes 196612
  7.2 171.0 %all-gather.7.cloned.1.call-start = ((), (), s32[]{:S(2)}) async-start(), calls=%async_computation | async-start | bytes 17039360 | tf_op jit(solution)/shard_map/all_gather | solution.py:17
  8.8 9.2 %copy-start.12 = (f32[2,128,8]{1,2,0:T(8,128)}, f32[2,128,8]{1,2,0:T(8,128)S(1)}, u32[]{:S(2)}) copy-start(f32[2,128,8]{1,2,0:T(8,128)S(1)} %get-tuple-element.170) | copy-start | bytes 24580
  9.4 8.6 %copy-start.11 = (f32[8,2,128]{2,0,1:T(8,128)}, f32[8,2,128]{2,0,1:T(8,128)S(1)}, u32[]{:S(2)}) copy-start(f32[8,2,128]{2,0,1:T(8,128)S(1)} %reduce_window_sum.24) | copy-start | bytes 24580
  9.6 8.4 %copy-start.14 = (f32[8,2]{0,1:T(2,128)}, f32[8,2]{0,1:T(2,128)S(1)}, u32[]{:S(2)}) copy-start(f32[8,2]{0,1:T(2,128)S(1)} %reduce_window_sum.26) | copy-start | bytes 196
  9.6 8.5 %copy-start.16 = (f32[8,1]{0,1:T(1,128)}, f32[8,1]{0,1:T(1,128)S(1)}, u32[]{:S(2)}) copy-start(f32[8,1]{0,1:T(1,128)S(1)} %get-tuple-element.179) | copy-start | bytes 100
  14.0 169.3 %copy-start.1 = (f32[2,128,8,64]{1,3,2,0:T(8,128)}, f32[2,128,8,64]{1,3,2,0:T(8,128)S(1)}, u32[]{:S(2)}) copy-start(f32[2,128,8,64]{1,3,2,0:T(8,128)S(1)} %copy.90) | copy-start | bytes 1572868
  14.4 0.8 copy-start.4
  18.1 202.4 %all-gather.9.cloned.1.call-start = ((), (), s32[]{:S(2)}) async-start(), calls=%async_computation.1 | async-start | bytes 17039360 | tf_op jit(solution)/shard_map/all_gather | solution.py:17
  19.3 4.1 copy-start.9
  23.4 151.9 %copy-start.2 = (bf16[2,128,8,64]{1,0,3,2:T(2,128)(2,1)}, bf16[2,128,8,64]{1,0,3,2:T(2,128)(2,1)S(1)}, u32[]{:S(2)}) copy-start(bf16[2,128,8,64]{1,0,3,2:T(2,128)(2,1)S(1)} %reshape.143) | copy-start | bytes 786436
  23.8 0.8 copy-start.6
  28.1 470.2 %all-reduce.5.cloned.1.call-start = ((), (), s32[]{:S(2)}) async-start(), calls=%async_computation.2 | async-start | bytes 10485760
  166.7 8.6 %copy-start.5 = (f32[2,8,64,128]{3,2,1,0:T(8,128)S(1)}, f32[2,8,64,128]{3,2,1,0:T(8,128)}, u32[]{:S(2)}) copy-start(f32[2,8,64,128]{3,2,1,0:T(8,128)} %copy-done.4) | copy-start | bytes 1572868
  166.7 8.6 %copy-start.13 = (f32[8,2]{1,0:T(8,128)S(1)}, f32[8,2]{1,0:T(8,128)}, u32[]{:S(2)}) copy-start(f32[8,2]{1,0:T(8,128)} %copy.95) | copy-start | bytes 196
  167.6 0.6 copy-start.15
  186.4 0.7 copy-start.7
  220.5 110.1 %copy-start.3 = (bf16[2,128,8,64]{1,0,3,2:T(2,128)(2,1)S(1)}, bf16[2,128,8,64]{1,0,3,2:T(2,128)(2,1)}, u32[]{:S(2)}) copy-start(bf16[2,128,8,64]{1,0,3,2:T(2,128)(2,1)} %copy-done.2) | copy-start | bytes 786436
  339.3 4.5 copy-start.10
Sparse Core Ops, SparseCore 0:
  18.1 101.8 all-gather.6
  123.4 97.0 all-gather.8
  224.1 274.1 all-reduce.4
